TPU v7x, 256 devices: a whole 4x4x8 slice. The times are simulated.
256 devices in a mesh: rep: 16 (over x_hi, z), head: 8 (over y, core), pair: 2 (over x_lo).
Axes of the slice: x: 4 (x_hi: 2, x_lo: 2; x = x_hi * 2 + x_lo), y: 4, z: 8, core: 2. Of those that a mesh axis runs over, the one named last changes fastest.
Arguments:
- queries: bfloat16 [384, 8192], P(('rep', 'pair'), 'head'), may hold values from -24 to 24
- new_keys: bfloat16 [384, 1024], P(('rep', 'pair'), 'head'), may hold values from -6 to 6
- new_values: bfloat16 [384, 1024], P(('rep', 'pair'), 'head'), may hold values from -6 to 6
- key_cache: bfloat16 [384, 1024, 1024], P(('rep', 'pair'), None, 'head'), may hold values from -6 to 6
- value_cache: bfloat16 [384, 1024, 1024], P(('rep', 'pair'), None, 'head'), may hold values from -6 to 6
- lengths: int32 [384], P(('rep', 'pair')), may hold values from 2 to 1024
- residual: bfloat16 [384, 8192], P('head', ('rep', 'pair')), may hold values from -36 to 36
- norm_gain: float32 [8192], replicated, may hold values from 0.5 to 1.5
- out_weight: bfloat16 [8192, 8192], P('head', ('rep', 'pair')), may hold values from -0.5 to 0.5
- gate_weight: bfloat16 [8192, 28672], P('head', ('rep', 'pair')), may hold values from -0.0625 to 0.0625
- up_weight: bfloat16 [8192, 28672], P('head', ('rep', 'pair')), may hold values from -0.0625 to 0.0625
- down_weight: bfloat16 [28672, 8192], P(('rep', 'pair'), 'head'), may hold values from -0.03125 to 0.03125
Outputs:
- hidden_state: bfloat16 [384, 8192], P('head', ('rep', 'pair'))
- ffn_out: bfloat16 [384, 8192], P(('rep', 'pair'), 'head')
Inputs may be any that keep to these rules, and one draw needn't show every extreme that they name: Cache slots 0 to lengths - 1 of a row are live, the others are ignored.
All inputs are finite; a program needn't handle non-finite values.
Results may differ from a plain program's by a relative error of at most 0.0095.
Values may be sent and summed in bfloat16 or wider, within the bound.
No kernel may reach another device: no remote copies, remote signals or barrier semaphores. Data moves between devices by JAX's collectives and lax.ppermute only.
A program may use at most 64 MiB of HBM per device.

v0:
```python
import jax
import jax.numpy as jnp
from jax import lax
from jax.sharding import PartitionSpec as P

HEADS = 64
KV_HEADS = 8
HEAD_DIM = 128


def sent_to_all(array, axis):
    copies = jnp.broadcast_to(array, (lax.axis_size(axis), *array.shape))
    return lax.all_to_all(copies, axis, split_axis=0, concat_axis=0, tiled=True)


def in_order(pieces, dim):
    dims = list(pieces.shape[1:])
    dims[dim] *= pieces.shape[0]
    return jnp.moveaxis(pieces, 0, dim).reshape(dims)


def gathered_copies(array, axis, dim):
    pieces = sent_to_all(array, axis)
    return in_order(pieces, dim)


def cut_along(array, dim, size):
    dims = array.shape
    pieces = array.reshape(*dims[:dim], size, dims[dim] // size, *dims[dim + 1 :])
    return jnp.moveaxis(pieces, dim, 0)


def sent_and_summed(array, axis, dim):
    size = lax.axis_size(axis)
    pieces = lax.all_to_all(cut_along(array, dim, size), axis, 0, 0, tiled=True)
    return jnp.sum(pieces, axis=0)


def side_by_side(arrays, axis, dim, along):
    both = jnp.concatenate(arrays, axis=along)
    filled, at, done = (sent_and_summed(both, axis, dim), 0, [])
    for a in arrays:
        done.append(lax.slice_in_dim(filled, at, at + a.shape[along], axis=along))
        at += a.shape[along]
    return tuple(done)


def local(
    queries,
    new_keys,
    new_values,
    key_cache,
    value_cache,
    lengths,
    residual,
    norm_gain,
    out_weight,
    gate_weight,
    up_weight,
    down_weight,
):
    row_count = queries.shape[0]
    slot_count = key_cache.shape[1]
    kv_local = key_cache.shape[2] // HEAD_DIM
    group_size = HEADS // KV_HEADS
    score_scale = HEAD_DIM ** (-0.5)
    query_heads = queries.reshape(row_count, kv_local, group_size, HEAD_DIM)
    cached_keys = key_cache.reshape(row_count, slot_count, kv_local, HEAD_DIM)
    cached_values = value_cache.reshape(row_count, slot_count, kv_local, HEAD_DIM)
    key_new = new_keys.reshape(row_count, kv_local, HEAD_DIM)
    value_new = new_values.reshape(row_count, kv_local, HEAD_DIM).astype(jnp.float32)
    scores = (
        jnp.einsum("rhgd,rchd->rhgc", query_heads, cached_keys, preferred_element_type=jnp.float32)
        * score_scale
    )
    slot_ids = lax.broadcasted_iota(jnp.int32, (row_count, 1, 1, slot_count), 3)
    live_mask = slot_ids < lengths[:, None, None, None]
    scores = jnp.where(live_mask, scores, -jnp.inf)
    own_score = (
        jnp.einsum("rhgd,rhd->rhg", query_heads, key_new, preferred_element_type=jnp.float32)
        * score_scale
    )
    row_top = jnp.maximum(jnp.max(scores, axis=3), own_score)
    weights = jnp.exp(scores - row_top[..., None])
    own_weight = jnp.exp(own_score - row_top)
    weight_total = jnp.sum(weights, axis=3) + own_weight
    weights_low = weights.astype(jnp.bfloat16)
    own_low = own_weight.astype(jnp.bfloat16).astype(jnp.float32)
    mixture = jnp.einsum(
        "rhgc,rchd->rhgd", weights_low, cached_values, preferred_element_type=jnp.float32
    )
    mixture = mixture + own_low[..., None] * value_new[:, :, None, :]
    attn = (mixture / weight_total[..., None]).astype(jnp.bfloat16).reshape(row_count, -1)
    projected_terms = jnp.dot(
        gathered_copies(attn, ("rep", "pair"), 0), out_weight, preferred_element_type=jnp.float32
    )
    projected = sent_and_summed(projected_terms, "head", 0)
    hidden_state = (residual.astype(jnp.float32) + projected).astype(jnp.bfloat16)
    full_rows = gathered_copies(hidden_state, ("rep", "pair"), 1)
    state_f = full_rows.astype(jnp.float32)
    mean_square = jnp.mean(state_f * state_f, axis=1, keepdims=True)
    normed = (state_f * lax.rsqrt(mean_square + 1e-05) * norm_gain).astype(jnp.bfloat16)
    normed_cols = lax.all_to_all(normed, "head", split_axis=1, concat_axis=0, tiled=True)
    gate_part = jnp.dot(normed_cols, gate_weight, preferred_element_type=jnp.float32)
    up_part = jnp.dot(normed_cols, up_weight, preferred_element_type=jnp.float32)
    gate_share, up_share = side_by_side((gate_part, up_part), "head", 1, 0)
    hidden_share = (jax.nn.silu(gate_share) * up_share).astype(jnp.bfloat16)
    hidden = gathered_copies(hidden_share, "head", 1)
    ffn_out = sent_and_summed(
        jnp.dot(hidden, down_weight, preferred_element_type=jnp.float32), ("rep", "pair"), 0
    )
    return (hidden_state, ffn_out.astype(jnp.bfloat16))


def solution(mesh):
    placed = (
        P(("rep", "pair"), "head"),
        P(("rep", "pair"), "head"),
        P(("rep", "pair"), "head"),
        P(("rep", "pair"), None, "head"),
        P(("rep", "pair"), None, "head"),
        P(("rep", "pair")),
        P("head", ("rep", "pair")),
        P(),
        P("head", ("rep", "pair")),
        P("head", ("rep", "pair")),
        P("head", ("rep", "pair")),
        P(("rep", "pair"), "head"),
    )
    return jax.shard_map(
        local,
        mesh=mesh,
        in_specs=placed,
        out_specs=(P("head", ("rep", "pair")), P(("rep", "pair"), "head")),
        check_vma=False,
    )
```

profile of v0, /device:TPU:32, one launch (start us, length us, event | category | flops | bytes accessed | tf_op | source)
XLA Modules:
  0.0 252.3 jit_solution(8546242657127766554)
XLA Ops:
  0.6 0.0 copy-start
  0.6 0.8 convert_element_type.54
  1.5 0.8 iota_compare_fusion
  2.3 0.8 copy.25
  3.1 0.8 fusion.14
  3.9 0.0 copy-done
  3.9 0.0 copy-start.1
  3.9 1.0 fusion.22
  4.9 0.2 fusion.9
  5.2 0.6 copy-done.1
  5.8 0.6 fusion.5
  6.4 0.1 broadcast_in_dim.30
  6.5 40.7 %all_to_all.46 = bf16[32,12,1024]{2,1,0:T(8,128)(2,1)} all-to-all(bf16[32,12,1024]{2,1,0:T(8,128)(2,1)S(1)} %broadcast_in_dim.30), channel_id=1, replica_groups=mesh['rep'=16,'head'=8,'pair'=2] {'rep','pair'}, dimensions={0} | all-to-all | bytes 1572864 | tf_op jit(solution)/shard_map/all_to_all | solution.py:13
  47.3 2.1 dot_general.28
  49.4 1.6 fusion.7
  51.0 13.2 %all_to_all.47 = f32[8,48,256]{2,1,0:T(8,128)S(1)} all-to-all(f32[8,48,256]{2,1,0:T(8,128)S(1)} %fusion.7), channel_id=1, replica_groups=mesh['rep'=16,'head'=8,'pair'=2] {'head'}, dimensions={0} | all-to-all | bytes 786432 | tf_op jit(solution)/shard_map/all_to_all | solution.py:35
  64.3 0.6 reduce_sum.46
  64.9 0.0 copy-start.3
  64.9 0.8 add_convert_fusion
  65.7 0.0 copy-start.2
  65.7 1.0 broadcast_in_dim.31
  66.7 4.7 %all-to-all-start.2 = ((bf16[32,48,256]{2,1,0:T(8,128)(2,1)}), bf16[32,48,256]{2,1,0:T(8,128)(2,1)}, u32[]{:S(2)}, u32[]{:S(2)}) async-start(bf16[32,48,256]{2,1,0:T(8,128)(2,1)} %broadcast_in_dim.31), calls=%async_computation.2 | async-start | bytes 1572864 | tf_op jit(solution)/shard_map/all_to_all | solution.py:13
  71.4 0.0 copy-done.3
  71.4 24.2 %all-to-all-done.2 = bf16[32,48,256]{2,1,0:T(8,128)(2,1)} async-done(((bf16[32,48,256]{2,1,0:T(8,128)(2,1)}), bf16[32,48,256]{2,1,0:T(8,128)(2,1)}, u32[]{:S(2)}, u32[]{:S(2)}) %all-to-all-start.2) | async-done | bytes 786464 | tf_op jit(solution)/shard_map/all_to_all | solution.py:13
  95.6 1.4 fusion.2
  97.0 1.3 convert_bitcast_fusion
  98.4 0.0 copy-done.2
  98.4 2.1 copy.17
  100.5 2.7 %reshape.129 = f32[48,8,1024]{2,1,0:T(8,128)} reshape(f32[48,32,256]{2,1,0:T(8,128)} %copy.17) | data formatting | bytes 3145728 | tf_op jit(solution)/shard_map/convert_element_type | solution.py:100
  103.1 1.6 multiply_convert_fusion
  104.7 0.0 copy-start.4
  104.7 0.4 copy.18
  105.2 15.8 %all_to_all.48 = bf16[48,8,1024]{2,0,1:T(8,128)(2,1)S(1)} all-to-all(bf16[48,8,1024]{2,0,1:T(8,128)(2,1)S(1)} %copy.18), channel_id=1, replica_groups=mesh['rep'=16,'head'=8,'pair'=2] {'head'}, dimensions={1} | all-to-all | bytes 1572864 | tf_op jit(solution)/shard_map/all_to_all | solution.py:103
  121.0 0.0 copy-done.4
  121.0 0.0 copy-start.5
  121.0 1.0 fusion.24
  122.0 0.5 copy-done.5
  122.5 1.0 fusion.23
  123.5 1.7 pad_maximum_fusion
  125.2 3.4 %copy.19 = f32[768,896]{0,1:T(8,128)} copy(f32[768,896]{1,0:T(8,128)} %pad_maximum_fusion) | data formatting | bytes 5505024 | tf_op jit(solution)/shard_map/concatenate | solution.py:40
  128.6 39.0 %all_to_all.49 = f32[8,768,112]{1,2,0:T(8,128)} all-to-all(f32[8,768,112]{1,2,0:T(8,128)} %bitcast.45), channel_id=1, replica_groups=mesh['rep'=16,'head'=8,'pair'=2] {'head'}, dimensions={0} | all-to-all | bytes 5505024 | tf_op jit(solution)/shard_map/all_to_all | solution.py:35
  167.6 2.0 reduce_sum.48
  169.6 0.1 fusion.13
  169.6 0.1 broadcast_in_dim.32
  169.7 15.2 %all_to_all.50 = bf16[8,384,112]{1,2,0:T(8,128)(2,1)} all-to-all(bf16[8,384,112]{1,2,0:T(8,128)(2,1)S(1)} %broadcast_in_dim.32), channel_id=1, replica_groups=mesh['rep'=16,'head'=8,'pair'=2] {'head'}, dimensions={0} | all-to-all | bytes 1376256 | tf_op jit(solution)/shard_map/all_to_all | solution.py:13
  184.9 2.4 copy.20
  187.4 2.6 %dot_general.32 = bf16[32,12,896]{2,1,0:T(8,128)(2,1)} reshape(bf16[384,8,112]{2,1,0:T(8,128)(2,1)} %copy.20) | data formatting | bytes 1376256 | tf_op jit(solution)/shard_map/dot_general | solution.py:110
  190.0 2.8 %fusion = f32[32,12,1024]{2,0,1:T(8,128)S(1)} fusion(bf16[896,1024]{1,0:T(8,128)(2,1)} %param.23, bf16[32,12,896]{2,1,0:T(8,128)(2,1)} %dot_general.32), kind=kOutput, calls=%fused_computation.3 | convolution fusion | flops 704643072 | bytes 4096000 | tf_op jit(solution)/shard_map/dot_general | solution.py:110
  192.8 0.9 copy.22
  193.7 56.3 %all_to_all.51 = f32[32,12,1024]{2,1,0:T(8,128)} all-to-all(f32[32,12,1024]{2,1,0:T(8,128)S(1)} %copy.22), channel_id=1, replica_groups=mesh['rep'=16,'head'=8,'pair'=2] {'rep','pair'}, dimensions={0} | all-to-all | bytes 3145728 | tf_op jit(solution)/shard_map/all_to_all | solution.py:35
  250.0 2.3 reduce_sum.49
  (6 shorter events, 0.1 us)
Async XLA Ops:
  0.6 3.3 %copy-start = (bf16[12,1024,128]{2,1,0:T(8,128)(2,1)S(1)}, bf16[12,1024,128]{2,1,0:T(8,128)(2,1)}, u32[]{:S(2)}) copy-start(bf16[12,1024,128]{2,1,0:T(8,128)(2,1)} %param.15) | copy-start | bytes 9437188
  3.9 1.9 copy-start.1
  64.9 6.5 %copy-start.3 = (f32[8192]{0:T(1024)S(1)}, f32[8192]{0:T(1024)}, u32[]{:S(2)}) copy-start(f32[8192]{0:T(1024)} %param.19) | copy-start | bytes 98308
  65.7 32.7 %copy-start.2 = (bf16[48,256]{1,0:T(8,128)(2,1)}, bf16[48,256]{1,0:T(8,128)(2,1)S(1)}, u32[]{:S(2)}) copy-start(bf16[48,256]{1,0:T(8,128)(2,1)S(1)} %add_convert_fusion) | copy-start | bytes 73732
  66.7 29.0 %all-to-all-start.2 = ((bf16[32,48,256]{2,1,0:T(8,128)(2,1)}), bf16[32,48,256]{2,1,0:T(8,128)(2,1)}, u32[]{:S(2)}, u32[]{:S(2)}) async-start(bf16[32,48,256]{2,1,0:T(8,128)(2,1)} %broadcast_in_dim.31), calls=%async_computation.2 | async-start | bytes 1572864 | tf_op jit(solution)/shard_map/all_to_all | solution.py:13
  104.7 16.3 %copy-start.4 = (bf16[1024,896]{1,0:T(8,128)(2,1)S(1)}, bf16[1024,896]{1,0:T(8,128)(2,1)}, u32[]{:S(2)}) copy-start(bf16[1024,896]{1,0:T(8,128)(2,1)} %param.22) | copy-start | bytes 5505028
  121.0 1.5 copy-start.5
where the time goes:
time: 253 us; the launch traced here: 252 us
  blocking collectives  180 us (71%)
  waiting for transfers between devices  24.2 us (10%)
  local copies, waits for them, and re-layouts  19.8 us (8%)
  other arithmetic  13.8 us (5%)
  matrix products  8.74 us (3%)
  starting transfers between devices  4.69 us (2%)
    all_to_all x3, blocking collectives, sent_and_summed(): pieces = lax.all_to_all(cut_along(array, dim, size), axis, 0, 0, tiled=True)  108 us
    all_to_all x2, blocking collectives, sent_to_all(): return lax.all_to_all(copies, axis, split_axis=0, concat_axis=0, tiled=True)  55.9 us
    all_to_all x1, waiting for transfers between devices, sent_to_all(): return lax.all_to_all(copies, axis, split_axis=0, concat_axis=0, tiled=True)  24.2 us
    all_to_all x1, blocking collectives, local(): lax.all_to_all(normed, 'head', split_axis=1, concat_axis=0, tiled=True)  15.8 us
  transfers between devices with their start and end apart: 1, of which 1 were waited for; matrix products, arithmetic and copies ran while one was open for 0% of the time, Pallas kernels for 0%

commit v1 on v0

--- a/solution.py
+++ b/solution.py
@@ -6,6 +6,12 @@
 HEADS = 64
 KV_HEADS = 8
 HEAD_DIM = 128
+
+
+def exchange_blocks(shard, mesh_axis, split, join):
+    pieces = jnp.split(shard, lax.axis_size(mesh_axis), axis=split)
+    received = lax.all_to_all(jnp.stack(pieces), mesh_axis, 0, 0)
+    return jnp.concatenate(received, axis=join)
 
 
 def sent_to_all(array, axis):
@@ -100,7 +106,7 @@
     state_f = full_rows.astype(jnp.float32)
     mean_square = jnp.mean(state_f * state_f, axis=1, keepdims=True)
     normed = (state_f * lax.rsqrt(mean_square + 1e-05) * norm_gain).astype(jnp.bfloat16)
-    normed_cols = lax.all_to_all(normed, "head", split_axis=1, concat_axis=0, tiled=True)
+    normed_cols = exchange_blocks(normed, "head", 1, 0)
     gate_part = jnp.dot(normed_cols, gate_weight, preferred_element_type=jnp.float32)
     up_part = jnp.dot(normed_cols, up_weight, preferred_element_type=jnp.float32)
     gate_share, up_share = side_by_side((gate_part, up_part), "head", 1, 0)

time: 253 us -> 243 us (0.960)
  blocking collectives: 180 us -> 208 us
  waiting for transfers between devices: 24.2 us -> 0 us
  local copies, waits for them, and re-layouts: 19.8 us -> 14.5 us
  starting transfers between devices: 4.69 us -> 0 us
  other arithmetic: 13.8 us -> 10.1 us
    all_to_all x2 -> x3, blocking collectives: 55.9 us -> 83.6 us  [sent_to_all(): return lax.all_to_all(copies, axis, split_axis=0, concat_axis=0, tiled=True)]
    all_to_all x1 -> x0, waiting for transfers between devices: 24.2 us -> none  [sent_to_all(): return lax.all_to_all(copies, axis, split_axis=0, concat_axis=0, tiled=True)]
    all_to_all x1 -> x0, starting transfers between devices: 4.69 us -> none  [sent_to_all(): return lax.all_to_all(copies, axis, split_axis=0, concat_axis=0, tiled=True)]
    convert_element_type x2 -> x1, local copies, waits for them, and re-layouts: 4.74 us -> 0.13 us  [local(): state_f = full_rows.astype(jnp.float32)]
  transfers between devices with their start and end apart: 1 -> 0, of which waited for: 1 -> 0; matrix products, arithmetic and copies ran while one was open for 0% -> 0% of each run, Pallas kernels for 0% -> 0%
where the time goes in v1:
time: 243 us; the launch traced here: 242 us
  blocking collectives  208 us (86%)
  local copies, waits for them, and re-layouts  14.5 us (6%)
  other arithmetic  10.1 us (4%)
  matrix products  8.72 us (4%)
    all_to_all x3, blocking collectives, sent_and_summed(): pieces = lax.all_to_all(cut_along(array, dim, size), axis, 0, 0, tiled=True)  108 us
    all_to_all x3, blocking collectives, sent_to_all(): return lax.all_to_all(copies, axis, split_axis=0, concat_axis=0, tiled=True)  83.6 us
    all_to_all x1, blocking collectives, exchange_blocks(): received = lax.all_to_all(jnp.stack(pieces), mesh_axis, 0, 0)  15.8 us
    reduce_sum x3, other arithmetic, sent_and_summed(): return jnp.sum(pieces, axis=0)  4.94 us

profile of v1, /device:TPU:32, one launch (start us, length us, event | category | flops | bytes accessed | tf_op | source)
XLA Modules:
  0.0 242.2 jit_solution(3939100175109274801)
XLA Ops:
  0.6 0.0 copy-start
  0.6 0.8 convert_element_type.52
  1.5 0.8 iota_compare_fusion
  2.3 0.8 copy.24
  3.1 0.8 fusion.22
  3.9 0.0 copy-done
  3.9 0.0 copy-start.1
  3.9 1.0 fusion.30
  4.9 0.2 fusion.9
  5.2 0.6 copy-done.1
  5.8 0.6 fusion.5
  6.4 0.1 broadcast_in_dim.30
  6.5 40.7 %all_to_all.35 = bf16[32,12,1024]{2,1,0:T(8,128)(2,1)} all-to-all(bf16[32,12,1024]{2,1,0:T(8,128)(2,1)S(1)} %broadcast_in_dim.30), channel_id=1, replica_groups=mesh['rep'=16,'head'=8,'pair'=2] {'rep','pair'}, dimensions={0} | all-to-all | bytes 1572864 | tf_op jit(solution)/shard_map/all_to_all | solution.py:19
  47.3 2.1 dot_general.28
  49.4 1.6 fusion.7
  51.0 13.2 %all_to_all.36 = f32[8,48,256]{2,1,0:T(8,128)S(1)} all-to-all(f32[8,48,256]{2,1,0:T(8,128)S(1)} %fusion.7), channel_id=1, replica_groups=mesh['rep'=16,'head'=8,'pair'=2] {'head'}, dimensions={0} | all-to-all | bytes 786432 | tf_op jit(solution)/shard_map/all_to_all | solution.py:41
  64.3 0.6 reduce_sum.46
  64.9 0.8 add_convert_fusion
  65.7 0.0 copy-start.2
  65.7 0.1 broadcast_in_dim.31
  65.8 27.7 %all_to_all.37 = bf16[32,48,256]{2,1,0:T(8,128)(2,1)S(1)} all-to-all(bf16[32,48,256]{2,1,0:T(8,128)(2,1)S(1)} %broadcast_in_dim.31), channel_id=1, replica_groups=mesh['rep'=16,'head'=8,'pair'=2] {'rep','pair'}, dimensions={0} | all-to-all | bytes 1572864 | tf_op jit(solution)/shard_map/all_to_all | solution.py:19
  93.4 0.3 fusion.2
  93.7 0.2 convert_bitcast_fusion
  93.9 0.0 copy-done.2
  93.9 0.0 copy-start.3
  93.9 0.1 copy.23
  94.1 0.6 copy-done.3
  94.7 0.2 multiply_convert_fusion
  94.9 0.0 copy-start.4
  95.0 15.8 %all_to_all.38 = bf16[8,48,1024]{2,1,0:T(8,128)(2,1)S(1)} all-to-all(bf16[8,48,1024]{2,1,0:T(8,128)(2,1)S(1)} %fusion.14), channel_id=1, replica_groups=mesh['rep'=16,'head'=8,'pair'=2] {'head'}, dimensions={0} | all-to-all | bytes 1572864 | tf_op jit(solution)/shard_map/all_to_all | solution.py:13
  110.8 0.0 copy-done.4
  110.8 0.0 copy-start.5
  110.8 1.0 fusion.32
  111.8 0.5 copy-done.5
  112.3 1.0 fusion.31
  113.3 1.7 pad_maximum_fusion
  115.1 3.4 %copy.17 = f32[768,896]{0,1:T(8,128)} copy(f32[768,896]{1,0:T(8,128)} %pad_maximum_fusion) | data formatting | bytes 5505024 | tf_op jit(solution)/shard_map/concatenate | solution.py:46
  118.4 39.0 %all_to_all.39 = f32[8,768,112]{1,2,0:T(8,128)} all-to-all(f32[8,768,112]{1,2,0:T(8,128)} %bitcast.77), channel_id=1, replica_groups=mesh['rep'=16,'head'=8,'pair'=2] {'head'}, dimensions={0} | all-to-all | bytes 5505024 | tf_op jit(solution)/shard_map/all_to_all | solution.py:41
  157.5 2.0 reduce_sum.48
  159.4 0.1 fusion.13
  159.5 0.1 broadcast_in_dim.32
  159.5 15.2 %all_to_all.40 = bf16[8,384,112]{1,2,0:T(8,128)(2,1)} all-to-all(bf16[8,384,112]{1,2,0:T(8,128)(2,1)S(1)} %broadcast_in_dim.32), channel_id=1, replica_groups=mesh['rep'=16,'head'=8,'pair'=2] {'head'}, dimensions={0} | all-to-all | bytes 1376256 | tf_op jit(solution)/shard_map/all_to_all | solution.py:19
  174.8 2.4 %copy.18 = bf16[384,8,112]{2,1,0:T(8,128)(2,1)} copy(bf16[384,8,112]{0,2,1:T(8,128)(2,1)} %bitcast.79) | data formatting | bytes 1376256 | tf_op jit(solution)/shard_map/transpose | solution.py:25
  177.2 2.6 %dot_general.32 = bf16[32,12,896]{2,1,0:T(8,128)(2,1)} reshape(bf16[384,8,112]{2,1,0:T(8,128)(2,1)} %copy.18) | data formatting | bytes 1376256 | tf_op jit(solution)/shard_map/dot_general | solution.py:116
  179.9 2.8 %fusion = f32[32,12,1024]{2,0,1:T(8,128)S(1)} fusion(bf16[896,1024]{1,0:T(8,128)(2,1)} %param.23, bf16[32,12,896]{2,1,0:T(8,128)(2,1)} %dot_general.32), kind=kOutput, calls=%fused_computation.3 | convolution fusion | flops 704643072 | bytes 4096000 | tf_op jit(solution)/shard_map/dot_general | solution.py:116
  182.6 0.9 copy.20
  183.6 56.3 %all_to_all.41 = f32[32,12,1024]{2,1,0:T(8,128)} all-to-all(f32[32,12,1024]{2,1,0:T(8,128)S(1)} %copy.20), channel_id=1, replica_groups=mesh['rep'=16,'head'=8,'pair'=2] {'rep','pair'}, dimensions={0} | all-to-all | bytes 3145728 | tf_op jit(solution)/shard_map/all_to_all | solution.py:41
  239.8 2.3 reduce_sum.49
  (13 shorter events, 0.1 us)
Async XLA Ops:
  0.6 3.3 %copy-start = (bf16[12,1024,128]{2,1,0:T(8,128)(2,1)S(1)}, bf16[12,1024,128]{2,1,0:T(8,128)(2,1)}, u32[]{:S(2)}) copy-start(bf16[12,1024,128]{2,1,0:T(8,128)(2,1)} %param.15) | copy-start | bytes 9437188
  3.9 1.9 copy-start.1
  65.7 28.2 %copy-start.2 = (bf16[48,256]{1,0:T(8,128)(2,1)}, bf16[48,256]{1,0:T(8,128)(2,1)S(1)}, u32[]{:S(2)}) copy-start(bf16[48,256]{1,0:T(8,128)(2,1)S(1)} %add_convert_fusion) | copy-start | bytes 73732
  93.9 0.8 copy-start.3
  94.9 15.9 %copy-start.4 = (bf16[1024,896]{1,0:T(8,128)(2,1)S(1)}, bf16[1024,896]{1,0:T(8,128)(2,1)}, u32[]{:S(2)}) copy-start(bf16[1024,896]{1,0:T(8,128)(2,1)} %param.22) | copy-start | bytes 5505028
  110.8 1.5 copy-start.5
